TPU v7x, 32 devices: a whole 2x2x4 slice. The times are simulated.
32 devices in a mesh: ctx: 8 (over y, x, core), ch: 4 (over z).
Axes of the slice: x: 2, y: 2, z: 4, core: 2. Of those that a mesh axis runs over, the one named last changes fastest.
Arguments:
- inputs: bfloat16 [1024, 1536], P('ctx', 'ch'), may hold values from -6 to 6
- grad_out: bfloat16 [1024, 1536], P('ctx', 'ch'), may hold values from -6 to 6
- filter_w: bfloat16 [12, 1024], P('ch', 'ctx'), may hold values from -6 to 6
Outputs:
- input_grad: bfloat16 [1024, 1536], P('ctx', 'ch')
- filter_grad: float32 [12, 1024], P('ch', 'ctx')
All inputs are finite; a program needn't handle non-finite values.
Results may differ from a plain program's by a relative error of at most 0.001.
Values may be sent and summed in bfloat16 or wider, within the bound.
No kernel may reach another device: no remote copies, remote signals or barrier semaphores. Data moves between devices by JAX's collectives and lax.ppermute only.
A program may use at most 64 MiB of HBM per device.

v0:
```python
import math

import jax
import jax.numpy as jnp
from jax import lax
from jax.sharding import PartitionSpec as P


def toeplitz_of(window, rows):
    heads = window.shape[0]
    reversed_window = window[:, ::-1]
    repeated = jnp.broadcast_to(reversed_window[:, None, :], (heads, rows, 2 * rows)).reshape(
        heads, 2 * rows * rows
    )
    skewed = repeated[:, : rows * (2 * rows - 1)].reshape(heads, rows, 2 * rows - 1)
    return skewed[:, :, rows - 1 : 2 * rows - 1]


def diagonal_terms(products, rows):
    heads = products.shape[0]
    flipped = products[:, :, ::-1]
    padded = jnp.pad(flipped, ((0, 0), (0, 0), (0, rows + 1)))
    sheared = padded.reshape(heads, rows * (2 * rows + 1))[:, : 2 * rows * rows].reshape(
        heads, rows, 2 * rows
    )
    diagonal_sums = jnp.sum(sheared, axis=1)
    return jnp.concatenate(
        [jnp.zeros((heads, 1), diagonal_sums.dtype), diagonal_sums[:, : 2 * rows - 1]], axis=1
    )


def body(inputs, grad_out, filter_w):
    rows = inputs.shape[0]
    heads = filter_w.shape[0]
    devices = lax.axis_size("ctx")
    tokens = rows * devices
    factor = float(tokens) ** (-0.5)
    position = lax.axis_index("ctx")
    input_heads = inputs.reshape(rows, heads, -1)
    input_start = jnp.zeros((rows, inputs.shape[1]), jnp.float32)
    gathered_filter = lax.all_gather(filter_w, "ctx", axis=1, tiled=True)
    extended_filter = jnp.concatenate(
        [jnp.zeros((heads, tokens), filter_w.dtype), gathered_filter], axis=1
    )
    wide_start = jnp.zeros((heads, 2 * tokens), jnp.float32)
    arrived = lax.all_gather(grad_out, "ctx", axis=0, tiled=True)
    blocks_in = arrived.shape[0] // rows
    group = math.gcd(blocks_in, 8)

    def absorb_group(group_index, totals):
        input_acc, wide_grad = totals
        slab = lax.dynamic_slice_in_dim(arrived, group_index * group * rows, group * rows, 0)
        slab = slab.reshape(group, rows, heads, -1)
        base = group_index * group - position
        lags = base + jnp.arange(group, dtype=jnp.int32)
        live = lags >= 0
        lag_blocks = lax.dynamic_slice_in_dim(
            extended_filter, (base - 1 + devices) * rows, (group + 1) * rows, 1
        )
        lag_blocks = lag_blocks.reshape(heads, group + 1, rows)
        windows = jnp.concatenate([lag_blocks[:, :-1], lag_blocks[:, 1:]], axis=2).transpose(
            1, 0, 2
        )
        windows = windows * live.astype(windows.dtype)[:, None, None]
        toeplitz = jax.vmap(lambda one: toeplitz_of(one, rows))(windows)
        contribution = jnp.einsum(
            "jgts,jtgc->sgc", toeplitz, slab, preferred_element_type=jnp.float32
        )
        input_acc = input_acc + contribution.reshape(rows, -1)
        products = jnp.einsum(
            "jtgc,sgc->jgts", slab, input_heads, preferred_element_type=jnp.float32
        )
        products = products * live.astype(jnp.float32)[:, None, None, None]
        window_grad = jax.vmap(lambda one: diagonal_terms(one, rows))(products)
        lower = window_grad[:, :, :rows].transpose(1, 0, 2).reshape(heads, group * rows)
        upper = window_grad[:, :, rows:].transpose(1, 0, 2).reshape(heads, group * rows)
        lower_start = (base - 1 + devices) * rows
        current = lax.dynamic_slice_in_dim(wide_grad, lower_start, group * rows, 1)
        wide_grad = lax.dynamic_update_slice_in_dim(wide_grad, current + lower, lower_start, 1)
        upper_start = (base + devices) * rows
        current = lax.dynamic_slice_in_dim(wide_grad, upper_start, group * rows, 1)
        wide_grad = lax.dynamic_update_slice_in_dim(wide_grad, current + upper, upper_start, 1)
        return (input_acc, wide_grad)

    input_acc, wide_grad = lax.fori_loop(
        0, blocks_in // group, absorb_group, (input_start, wide_start)
    )
    filter_terms = wide_grad[:, tokens:]
    filter_sum = lax.psum_scatter(filter_terms, "ctx", scatter_dimension=1, tiled=True)
    input_grad = (input_acc * factor).astype(jnp.bfloat16)
    filter_grad = filter_sum * factor
    return (input_grad, filter_grad)


def solution(mesh):
    placed = (P("ctx", "ch"), P("ctx", "ch"), P("ch", "ctx"))
    return jax.shard_map(
        body,
        mesh=mesh,
        in_specs=placed,
        out_specs=(P("ctx", "ch"), P("ch", "ctx")),
        check_vma=False,
    )
```

profile of v0, /device:TPU:0, one launch (start us, length us, event | category | flops | bytes accessed | tf_op | source)
XLA Modules:
  0.0 75.6 jit_solution(6313740836334110728)
XLA Ops:
  7.2 0.0 reduce-scatter.4.cloned.1.call-start
  7.2 1.0 %copy.17 = bf16[128,384]{0,1:T(8,128)(2,1)S(1)} copy(bf16[128,384]{1,0:T(8,128)(2,1)} %param.3) | data formatting | bytes 196608 | tf_op args[0]
  8.2 12.2 %all_gather.7 = bf16[1024,384]{1,0:T(8,128)(2,1)S(1)} all-gather(bf16[128,384]{1,0:T(8,128)(2,1)} %param.4), channel_id=1, replica_groups=mesh['ctx'=8,'ch'=4] {'ctx'}, dimensions={0}, use_global_device_ids=true | all-gather | bytes 884736 | tf_op jit(solution)/shard_map/all_gather | solution.py:46
  20.5 0.2 reshape.70
  20.7 0.0 copy-start
  20.7 1.0 %copy-done = bf16[8,128,3,128]{3,2,1,0:T(4,128)(2,1)} copy-done((bf16[8,128,3,128]{3,2,1,0:T(4,128)(2,1)}, bf16[8,128,3,128]{3,2,1,0:T(4,128)(2,1)S(1)}, u32[]{:S(2)}) %copy-start) | copy-done | bytes 786456
  21.8 0.4 multiply_bitcast_fusion
  22.2 0.7 rev.9
  22.9 0.5 copy.28
  23.3 2.7 %pad.7.clone = f32[8,3,128,257]{3,2,0,1:T(8,128)} pad(f32[8,3,128,128]{3,2,0,1:T(8,128)S(1)} %copy.28, f32[]{:T(128)} %constant.39.clone.1), padding=0_0x0_0x0_0x0_129 | pad | bytes 4730884 | tf_op jit(solution)/shard_map/while/body/eval_jaxpr/vmap(jit(_pad))/pad | solution.py:22
  26.0 4.3 %reshape.62 = f32[8,3,32896]{2,0,1:T(8,128)S(1)} reshape(f32[8,3,128,257]{3,2,0,1:T(8,128)} %pad.7.clone) | data formatting | bytes 6316032 | tf_op jit(solution)/shard_map/while/body/eval_jaxpr/vmap()/reshape | solution.py:23
  30.3 0.2 slice.49
  30.5 0.0 copy-start.2
  30.5 0.9 %bitcast_reduce_fusion = f32[8,3,256]{2,0,1:T(8,128)S(1)} fusion(f32[3,8,128,256]{3,1,2,0:T(8,128)S(1)} %bitcast.49), kind=kLoop, calls=%fused_computation | loop fusion | flops 780288 | bytes 3170304 | tf_op jit(solution)/shard_map/while/body/eval_jaxpr/vmap()/reduce_sum | solution.py:26
  31.4 0.1 slice_bitcast_fusion
  31.5 0.1 fusion.6
  31.6 1.0 %copy.26 = f32[3,1024]{0,1:T(8,128)} copy(f32[3,1024]{1,0:T(4,128)S(1)} %slice.52) | data formatting | bytes 24576
  32.7 0.0 reduce-scatter.4.cloned.1.call-update
  32.7 0.0 copy-done.2
  32.7 8.6 %all_gather.6 = bf16[3,1024]{1,0:T(4,128)(2,1)S(1)} all-gather(bf16[3,128]{1,0:T(4,128)(2,1)S(1)} %copy-done.2), channel_id=1, replica_groups=mesh['ctx'=8,'ch'=4] {'ctx'}, dimensions={1}, use_global_device_ids=true | all-gather | bytes 6912 | tf_op jit(solution)/shard_map/all_gather | solution.py:41
  41.4 0.1 fusion.7
  41.4 0.2 rev.8
  41.6 0.1 broadcast_in_dim.19
  41.7 0.1 slice.47
  41.8 0.0 copy-start.1
  41.8 6.0 %reshape.59 = bf16[8,3,128,255]{3,2,0,1:T(8,128)(2,1)} reshape(bf16[8,3,32640]{2,0,1:T(8,128)(2,1)S(1)} %slice.47) | data formatting | bytes 3133440 | tf_op jit(solution)/shard_map/while/body/eval_jaxpr/vmap()/reshape | solution.py:15
  47.8 0.0 copy-done.1
  47.8 2.1 %fusion.1 = bf16[3,128,128]{1,2,0:T(8,128)(2,1)S(1)} fusion(bf16[8,3,128,255]{3,2,0,1:T(8,128)(2,1)} %reshape.59, bf16[8,128,3,128]{3,2,1,0:T(4,128)(2,1)S(1)} %copy-done.1), kind=kOutput, calls=%fused_computation.4 | convolution fusion | flops 100761600 | bytes 1671168 | tf_op jit(solution)/shard_map/while/body/eval_jaxpr/jgts,jtgc->sgc/dot_general | solution.py:66
  49.9 0.8 copy.21
  50.7 16.6 %reduce-scatter.4.cloned.1.call-done = f32[128,3]{1,0:T(8,128)} async-done(((f32[1024,3]{1,0:T(8,128)}), f32[128,3]{1,0:T(8,128)}) %reduce-scatter.4.cloned.1.call-update) | async-done | bytes 1552
  67.2 0.9 %copy.27 = f32[3,128]{1,0:T(4,128)S(1)} copy(f32[3,128]{0,1:T(8,128)} %bitcast.55) | data formatting | bytes 3072
  68.1 0.6 broadcast_multiply_fusion
  (9 shorter events, 0.1 us)
Async XLA Ops:
  7.2 60.1 %reduce-scatter.4.cloned.1.call-start = ((), (), s32[]{:S(2)}) async-start(), calls=%async_computation.1 | async-start | bytes 589824
  20.7 1.0 %copy-start = (bf16[8,128,3,128]{3,2,1,0:T(4,128)(2,1)}, bf16[8,128,3,128]{3,2,1,0:T(4,128)(2,1)S(1)}, u32[]{:S(2)}) copy-start(bf16[8,128,3,128]{3,2,1,0:T(4,128)(2,1)S(1)} %reshape.70) | copy-start | bytes 2359300
  30.5 2.2 %copy-start.2 = (bf16[3,128]{1,0:T(4,128)(2,1)S(1)}, bf16[3,128]{1,0:T(4,128)(2,1)}, u32[]{:S(2)}) copy-start(bf16[3,128]{1,0:T(4,128)(2,1)} %param.5) | copy-start | bytes 2308
  41.8 6.0 %copy-start.1 = (bf16[8,128,3,128]{3,2,1,0:T(4,128)(2,1)S(1)}, bf16[8,128,3,128]{3,2,1,0:T(4,128)(2,1)}, u32[]{:S(2)}) copy-start(bf16[8,128,3,128]{3,2,1,0:T(4,128)(2,1)} %copy-done) | copy-start | bytes 2359300
Sparse Core Ops, SparseCore 0:
  32.8 34.3 reduce-scatter.3
where the time goes:
time: 75.9 us; the launch traced here: 75.6 us
  blocking collectives  20.8 us (27%)
  local copies, waits for them, and re-layouts  19.9 us (26%)
  waiting for transfers between devices  16.6 us (22%)
  between operations  14.2 us (19%)
  matrix products  2.49 us (3%)
  other arithmetic  1.58 us (2%)
    unnamed x2, waiting for transfers between devices  16.6 us
    all_gather x1, blocking collectives, body(): arrived = lax.all_gather(grad_out, 'ctx', axis=0, tiled=True)  12.2 us
    all_gather x1, blocking collectives, body(): gathered_filter = lax.all_gather(filter_w, 'ctx', axis=1, tiled=True)  8.56 us
    reshape x1, local copies, waits for them, and re-layouts, toeplitz_of(): repeated[:, :rows * (2 * rows - 1)].reshape(heads, rows, 2 * rows - 1)  6.01 us
    unnamed x13, local copies, waits for them, and re-layouts  5.33 us
    reshape x1, local copies, waits for them, and re-layouts, diagonal_terms(): padded.reshape(heads, rows * (2 * rows + 1))[:, :2 * rows * rows]  4.31 us
    pad x1, local copies, waits for them, and re-layouts, diagonal_terms(): padded = jnp.pad(flipped, ((0, 0), (0, 0), (0, rows + 1)))  2.67 us
    dot_general x1, matrix products, absorb_group(): jnp.einsum('jgts,jtgc->sgc', toeplitz, slab, preferred_element_type=jnp.f...  2.08 us
  transfers between devices with their start and end apart: 1, of which 1 were waited for; matrix products, arithmetic and copies ran while one was open for 12% of the time, Pallas kernels for 0%

commit v1 on v0

v1 whole, which is shorter than its diff:
```python
import functools

import jax
import jax.numpy as jnp
from jax import lax
from jax.experimental import pallas as pl
from jax.experimental.pallas import tpu as pltpu
from jax.sharding import PartitionSpec as P

EXTRA = 8
VMEM = pltpu.VMEM


def pack_kernel(grad_ref, input_ref, filter_ref, out_ref, filter_vmem, sems):
    rows = grad_ref.shape[0]
    heads = filter_ref.shape[0]
    width = filter_ref.shape[1]
    copies = [
        pltpu.make_async_copy(filter_ref, filter_vmem, sems.at[0]),
        pltpu.make_async_copy(grad_ref, out_ref.at[pl.ds(0, rows)], sems.at[1]),
        pltpu.make_async_copy(input_ref, out_ref.at[pl.ds(rows, rows)], sems.at[2]),
    ]
    for copy in copies:
        copy.start()
    copies[0].wait()
    block = filter_vmem[...].astype(jnp.float32)
    block = jnp.concatenate([block, jnp.zeros((EXTRA - heads, width), jnp.float32)], axis=0)
    out_ref[2 * rows :, :width] = block.astype(out_ref.dtype)
    out_ref[2 * rows :, width:] = jnp.zeros((EXTRA, out_ref.shape[1] - width), out_ref.dtype)
    copies[1].wait()
    copies[2].wait()


def repeat(count, step, start):
    if count <= 4:
        for index in range(count):
            start = step(index, start)
        return start
    return lax.fori_loop(0, count, step, start)


def main_kernel(heads, factor, mine_ref, theirs_ref, out_ref, terms_ref, lags_ref, toeplitz_ref, out_vmem, terms_vmem, sems):
    half, span, channels = mine_ref.shape
    rows = (span - EXTRA) // 2
    width = channels // heads
    blocks = 2 * half
    position = lax.axis_index("ctx")
    pair = position // 2
    core = position - 2 * pair

    lags_ref[...] = jnp.zeros_like(lags_ref)

    def place(slot, carry):
        for ref, parity in ((mine_ref, core), (theirs_ref, 1 - core)):
            at = pl.multiple_of((blocks + 1 + 2 * slot + parity) * rows, rows)
            lags_ref[:, pl.ds(at, rows)] = ref[slot, 2 * rows :, :rows].astype(jnp.float32)
        return carry

    repeat(half, place, 0)
    start = pl.multiple_of((blocks - position) * rows, rows)
    window = lags_ref[:, pl.ds(start, (blocks + 1) * rows)]
    reach = (blocks + 1) * rows
    for head in range(heads):
        lines = jnp.broadcast_to(window[head : head + 1], (rows, reach))
        skewed = pltpu.roll(lines, 0, 1, stride=1, stride_axis=0)
        toeplitz_ref[head] = skewed[:, rows:].astype(toeplitz_ref.dtype)

    def compute(even_ref, odd_ref, parity):
        for head in range(heads):
            lanes = slice(head * width, (head + 1) * width)

            def accumulate(slot, total):
                both = jnp.concatenate([even_ref[slot, :rows, lanes], odd_ref[slot, :rows, lanes]], axis=0)
                at = slot * 2 * rows if isinstance(slot, int) else pl.multiple_of(slot * 2 * rows, 2 * rows)
                return total + jnp.dot(
                    toeplitz_ref[head, :, pl.ds(at, 2 * rows)], both, preferred_element_type=jnp.float32
                )

            total = repeat(half, accumulate, jnp.zeros((rows, width), jnp.float32))
            out_vmem[:, lanes] = (total * factor).astype(out_vmem.dtype)
            pltpu.make_async_copy(out_vmem.at[:, lanes], out_ref.at[:, lanes], sems.at[head]).start()

        sums = []
        for head in range(heads):
            lanes = slice(head * width, (head + 1) * width)

            def grad_at(ref, slot):
                held = ref[jnp.minimum(slot, half - 1), :rows, lanes]
                return jnp.where(slot < half, held, jnp.zeros_like(held))

            def accumulate(slot, total):
                mid = slot + pair
                if parity == 0:
                    first, second, third = grad_at(even_ref, mid), grad_at(odd_ref, mid), grad_at(even_ref, mid + 1)
                else:
                    first, second, third = grad_at(odd_ref, mid), grad_at(even_ref, mid + 1), grad_at(odd_ref, mid + 1)
                left = jnp.concatenate(
                    [even_ref[slot, rows : 2 * rows, lanes], odd_ref[slot, rows : 2 * rows, lanes]], axis=1
                )
                right = jnp.concatenate(
                    [jnp.concatenate([first, second], axis=1), jnp.concatenate([second, third], axis=1)], axis=0
                )
                return total + lax.dot_general(
                    left, right, (((1,), (1,)), ((), ())), preferred_element_type=jnp.float32
                )

            products = repeat(half, accumulate, jnp.zeros((rows, 2 * rows), jnp.float32))
            folded = products[0:8]
            for group in range(1, rows // 8):
                folded = folded + pltpu.roll(products[8 * group : 8 * group + 8], 2 * rows - 8 * group, 1)
            sums.append(folded)
        folded = jnp.concatenate(sums, axis=0)
        line = lax.broadcasted_iota(jnp.int32, folded.shape, 0)
        for bit in (1, 2, 4):
            folded = jnp.where((line & bit) != 0, pltpu.roll(folded, 2 * rows - bit, 1), folded)
        for head in range(heads):
            terms_vmem[head : head + 1, :] = (
                jnp.sum(folded[8 * head : 8 * head + 8, :rows], axis=0, keepdims=True) * factor
            )

    @pl.when(core == 0)
    def _():
        compute(mine_ref, theirs_ref, 0)

    @pl.when(core == 1)
    def _():
        compute(theirs_ref, mine_ref, 1)

    last = pltpu.make_async_copy(terms_vmem, terms_ref, sems.at[heads])
    last.start()
    for head in range(heads):
        lanes = slice(head * width, (head + 1) * width)
        pltpu.make_async_copy(out_vmem.at[:, lanes], out_ref.at[:, lanes], sems.at[head]).wait()
    last.wait()


def body(inputs, grad_out, filter_w):
    rows, channels = inputs.shape
    heads = filter_w.shape[0]
    blocks = lax.axis_size("ctx")
    half = blocks // 2
    factor = float(rows * blocks) ** (-0.5)
    anywhere = pl.BlockSpec(memory_space=pl.ANY)
    on_chip = pl.BlockSpec(memory_space=VMEM)
    span = 2 * rows + EXTRA
    payload = pl.pallas_call(
        pack_kernel,
        out_shape=jax.ShapeDtypeStruct((span, channels), inputs.dtype),
        in_specs=[anywhere] * 3,
        out_specs=on_chip,
        scratch_shapes=[VMEM(filter_w.shape, filter_w.dtype), pltpu.SemaphoreType.DMA((3,))],
        name="pack",
    )(grad_out, inputs, filter_w)
    groups = [[2 * slot + core for slot in range(half)] for core in range(2)]
    mine = lax.all_gather(payload, "ctx", axis=0, tiled=False, axis_index_groups=groups)
    theirs = lax.ppermute(mine, "ctx", [(index, index ^ 1) for index in range(blocks)])
    return pl.pallas_call(
        functools.partial(main_kernel, heads, factor),
        out_shape=(
            jax.ShapeDtypeStruct((rows, channels), inputs.dtype),
            jax.ShapeDtypeStruct((heads, rows), jnp.float32),
        ),
        in_specs=[on_chip] * 2,
        out_specs=(anywhere, anywhere),
        scratch_shapes=[
            VMEM((EXTRA, (2 * blocks + 1) * rows), jnp.float32),
            VMEM((heads, rows, blocks * rows), inputs.dtype),
            VMEM((rows, channels), inputs.dtype),
            VMEM((heads, rows), jnp.float32),
            pltpu.SemaphoreType.DMA((heads + 1,)),
        ],
        name="main",
    )(mine, theirs)


def solution(mesh):
    placed = (P("ctx", "ch"), P("ctx", "ch"), P("ch", "ctx"))
    return jax.shard_map(
        body,
        mesh=mesh,
        in_specs=placed,
        out_specs=(P("ctx", "ch"), P("ch", "ctx")),
        check_vma=False,
    )
```

time: 75.9 us -> 23.3 us (0.31)
  local copies, waits for them, and re-layouts: 19.9 us -> 0.9 us
  waiting for transfers between devices: 16.6 us -> 2.32 us
  between operations: 14.2 us -> 0.64 us
  blocking collectives: 20.8 us -> 14.1 us
  Pallas kernels: 0 us -> 5.14 us
  matrix products: 2.49 us -> 0 us
  other arithmetic: 1.58 us -> 0 us
    unnamed x2 -> x0, waiting for transfers between devices: 16.6 us -> none
    reshape x4 -> x0, local copies, waits for them, and re-layouts: 10.6 us -> none  [the longest x1 6.01 us: toeplitz_of(): repeated[:, :rows * (2 * rows - 1)].reshape(heads, rows, 2 * rows - 1)]
    all_gather x2 -> x1, blocking collectives: 20.8 us -> 14.1 us  [body(): lax.all_gather(payload, 'ctx', axis=0, tiled=False, axis_index_groups=gro...]
    pallas_call x0 -> x2, Pallas kernels: none -> 5.14 us  [the longest x1 3.49 us: body(): pl.pallas_call(functools.partial(main_kernel, heads, factor), out_shape=(...]
    unnamed x13 -> x4, local copies, waits for them, and re-layouts: 5.33 us -> 0.9 us
    pad x1 -> x0, local copies, waits for them, and re-layouts: 2.67 us -> none  [diagonal_terms(): padded = jnp.pad(flipped, ((0, 0), (0, 0), (0, rows + 1)))]
    dot_general x2 -> x0, matrix products: 2.49 us -> none  [the longest x1 2.08 us: absorb_group(): jnp.einsum('jgts,jtgc->sgc', toeplitz, slab, preferred_element_type=jnp.f...]
    ppermute x0 -> x1, waiting for transfers between devices: none -> 2.32 us  [body(): lax.ppermute(mine, 'ctx', [(index, index ^ 1) for index in range(blocks)])]
  transfers between devices with their start and end apart: 1 -> 1, of which waited for: 1 -> 1; matrix products, arithmetic and copies ran while one was open for 12% -> 0% of each run, Pallas kernels for 0% -> 0%
where the time goes in v1:
time: 23.3 us; the launch traced here: 23.1 us
  blocking collectives  14.1 us (61%)
  Pallas kernels  5.14 us (22%)
  waiting for transfers between devices  2.32 us (10%)
  local copies, waits for them, and re-layouts  0.9 us (4%)
  between operations  0.64 us (3%)
    all_gather x1, blocking collectives, body(): lax.all_gather(payload, 'ctx', axis=0, tiled=False, axis_index_groups=gro...  14.1 us
    pallas_call x1, Pallas kernels, body(): pl.pallas_call(functools.partial(main_kernel, heads, factor), out_shape=(...  3.49 us
    ppermute x1, waiting for transfers between devices, body(): lax.ppermute(mine, 'ctx', [(index, index ^ 1) for index in range(blocks)])  2.32 us
    pallas_call x1, Pallas kernels, body(): pl.pallas_call(pack_kernel, out_shape=jax.ShapeDtypeStruct((span, channel...  1.65 us
    unnamed x4, local copies, waits for them, and re-layouts  0.9 us
  transfers between devices with their start and end apart: 1, of which 1 were waited for; matrix products, arithmetic and copies ran while one was open for 0% of the time, Pallas kernels for 0%

profile of v1, /device:TPU:0, one launch (start us, length us, event | category | flops | bytes accessed | tf_op | source)
XLA Modules:
  0.0 23.1 jit_solution(8542390656183662164)
XLA Ops:
  0.6 1.6 %pack.1 = bf16[264,384]{1,0:T(8,128)(2,1)} custom-call(bf16[128,384]{1,0:T(8,128)(2,1)} %grad_ref.1, bf16[128,384]{1,0:T(8,128)(2,1)} %input_ref.1, bf16[3,128]{1,0:T(4,128)(2,1)} %filter_ref.1), custom_call_target="tpu_custom_call" | custom-call | tf_op jit(solution)/shard_map/pack/pallas_call | solution.py:146
  2.3 14.1 %all-gather = bf16[1056,384]{1,0:T(8,128)(2,1)S(1)} all-gather(bf16[264,384]{1,0:T(8,128)(2,1)} %pack.1), channel_id=2, replica_groups={{0,8,16,24},{4,12,20,28},{1,9,17,25},{5,13,21,29},{2,10,18,26},{6,14,22..., dimensions={0}, use_global_device_ids=true | all-gather | bytes 1013760 | tf_op jit(solution)/shard_map/all_gather | solution.py:155
  16.4 0.0 copy-start
  16.4 0.0 collective-permute-start
  16.4 2.3 %collective-permute-done.theirs_ref = bf16[4,264,384]{2,1,0:T(8,128)(2,1)S(1)} collective-permute-done((bf16[4,264,384]{2,1,0:T(8,128)(2,1)S(1)}, bf16[4,264,384]{2,1,0:T(8,128)(2,1)S(1)}, u32[]{:S(2)}, u32[]{:S(2)}) %collective-permute-start) | collective-permute-done | bytes 811040 | tf_op jit(solution)/shard_map/ppermute | solution.py:156
  18.7 0.0 copy-done
  18.7 0.0 copy-start.1
  18.7 0.9 %copy-done.1 = bf16[4,264,384]{2,1,0:T(8,128)(2,1)} copy-done((bf16[4,264,384]{2,1,0:T(8,128)(2,1)}, bf16[4,264,384]{2,1,0:T(8,128)(2,1)S(1)}, u32[]{:S(2)}) %copy-start.1) | copy-done | bytes 811032
  19.6 3.5 %main.1 = (bf16[128,384]{1,0:T(8,128)(2,1)}, f32[3,128]{1,0:T(4,128)}) custom-call(bf16[4,264,384]{2,1,0:T(8,128)(2,1)} %bitcast.2, bf16[4,264,384]{2,1,0:T(8,128)(2,1)} %copy-done.1), custom_call_target="tpu_custom_call" | custom-call | tf_op jit(solution)/shard_map/main/pallas_call | solution.py:157
Async XLA Ops:
  16.4 2.3 %copy-start = (bf16[1056,384]{1,0:T(8,128)(2,1)}, bf16[1056,384]{1,0:T(8,128)(2,1)S(1)}, u32[]{:S(2)}) copy-start(bf16[1056,384]{1,0:T(8,128)(2,1)S(1)} %all-gather) | copy-start | bytes 2433028
  16.4 2.3 %collective-permute-start = (bf16[4,264,384]{2,1,0:T(8,128)(2,1)S(1)}, bf16[4,264,384]{2,1,0:T(8,128)(2,1)S(1)}, u32[]{:S(2)}, u32[]{:S(2)}) collective-permute-start(bf16[4,264,384]{2,1,0:T(8,128)(2,1)S(1)} %bitcast.1), channel_id=1, source_target_pairs={{0,4},{4,0},{8,12},{12,8},{16,20},{20,16},{24,28},{28,24},{1,5},{5... | collective-permute-start | bytes 2433032 | tf_op jit(solution)/shard_map/ppermute | solution.py:156
  18.7 0.9 %copy-start.1 = (bf16[4,264,384]{2,1,0:T(8,128)(2,1)}, bf16[4,264,384]{2,1,0:T(8,128)(2,1)S(1)}, u32[]{:S(2)}) copy-start(bf16[4,264,384]{2,1,0:T(8,128)(2,1)S(1)} %collective-permute-done.theirs_ref) | copy-start | bytes 2433028

commit v2 on v1

--- a/solution.py
+++ b/solution.py
@@ -134,6 +134,10 @@
     last.wait()
 
 
+def limit(size):
+    return min(size + (4 << 20), 60 << 20)
+
+
 def body(inputs, grad_out, filter_w):
     rows, channels = inputs.shape
     heads = filter_w.shape[0]
@@ -146,11 +150,13 @@
     payload = pl.pallas_call(
         pack_kernel,
         out_shape=jax.ShapeDtypeStruct((span, channels), inputs.dtype),
-        in_specs=[anywhere] * 3,
+        in_specs=[pl.BlockSpec(memory_space=pltpu.HBM)] * 3,
         out_specs=on_chip,
         scratch_shapes=[VMEM(filter_w.shape, filter_w.dtype), pltpu.SemaphoreType.DMA((3,))],
+        compiler_params=pltpu.CompilerParams(vmem_limit_bytes=limit(3 * span * channels * 2)),
         name="pack",
-    )(grad_out, inputs, filter_w)
+    )(*(pltpu.with_memory_space_constraint(each, pltpu.HBM) for each in (grad_out, inputs, filter_w)))
+    scratch = 4 * EXTRA * (2 * blocks + 1) * rows + 2 * heads * rows * blocks * rows + 8 * rows * channels
     groups = [[2 * slot + core for slot in range(half)] for core in range(2)]
     mine = lax.all_gather(payload, "ctx", axis=0, tiled=False, axis_index_groups=groups)
     theirs = lax.ppermute(mine, "ctx", [(index, index ^ 1) for index in range(blocks)])
@@ -169,6 +175,7 @@
             VMEM((heads, rows), jnp.float32),
             pltpu.SemaphoreType.DMA((heads + 1,)),
         ],
+        compiler_params=pltpu.CompilerParams(vmem_limit_bytes=limit(scratch)),
         name="main",
     )(mine, theirs)
 

time: 23.3 us -> 19.1 us (0.82)
  Pallas kernels: 5.14 us -> 3.09 us
  blocking collectives: 14.1 us -> 12.9 us
  local copies, waits for them, and re-layouts: 0.9 us -> 0 us
    pallas_call x1, Pallas kernels: 3.49 us -> 2.11 us  [body(): pl.pallas_call(functools.partial(main_kernel, heads, factor), out_shape=(...]
    all_gather x1, blocking collectives: 14.1 us -> 12.9 us  [body(): lax.all_gather(payload, 'ctx', axis=0, tiled=False, axis_index_groups=gro...]
    unnamed x4 -> x0, local copies, waits for them, and re-layouts: 0.9 us -> none
    pallas_call x1, Pallas kernels: 1.65 us -> 0.98 us  [body(): pl.pallas_call(pack_kernel, out_shape=jax.ShapeDtypeStruct((span, channel...]
where the time goes in v2:
time: 19.1 us; the launch traced here: 18.9 us
  blocking collectives  12.9 us (68%)
  Pallas kernels  3.09 us (16%)
  waiting for transfers between devices  2.32 us (12%)
  between operations  0.64 us (3%)
    all_gather x1, blocking collectives, body(): lax.all_gather(payload, 'ctx', axis=0, tiled=False, axis_index_groups=gro...  12.9 us
    ppermute x1, waiting for transfers between devices, body(): lax.ppermute(mine, 'ctx', [(index, index ^ 1) for index in range(blocks)])  2.32 us
    pallas_call x1, Pallas kernels, body(): pl.pallas_call(functools.partial(main_kernel, heads, factor), out_shape=(...  2.11 us
    pallas_call x1, Pallas kernels, body(): pl.pallas_call(pack_kernel, out_shape=jax.ShapeDtypeStruct((span, channel...  0.98 us
  transfers between devices with their start and end apart: 1, of which 1 were waited for; matrix products, arithmetic and copies ran while one was open for 0% of the time, Pallas kernels for 0%

profile of v2, /device:TPU:0, one launch (start us, length us, event | category | flops | bytes accessed | tf_op | source)
XLA Modules:
  0.0 18.9 jit_solution(6598029746318080392)
XLA Ops:
  0.6 1.0 %pack.1 = bf16[264,384]{1,0:T(8,128)(2,1)S(1)} custom-call(bf16[128,384]{1,0:T(8,128)(2,1)} %grad_ref.1, bf16[128,384]{1,0:T(8,128)(2,1)} %input_ref.1, bf16[3,128]{1,0:T(4,128)(2,1)} %filter_ref.1), custom_call_target="tpu_custom_call" | custom-call | tf_op jit(solution)/shard_map/pack/pallas_call | solution.py:150
  1.6 12.9 %all-gather = bf16[1056,384]{1,0:T(8,128)(2,1)S(1)} all-gather(bf16[264,384]{1,0:T(8,128)(2,1)S(1)} %pack.1), channel_id=2, replica_groups={{0,8,16,24},{4,12,20,28},{1,9,17,25},{5,13,21,29},{2,10,18,26},{6,14,22..., dimensions={0}, use_global_device_ids=true | all-gather | bytes 1013760 | tf_op jit(solution)/shard_map/all_gather | solution.py:161
  14.5 0.0 collective-permute-start
  14.5 2.3 %collective-permute-done.theirs_ref = bf16[4,264,384]{2,1,0:T(8,128)(2,1)S(1)} collective-permute-done((bf16[4,264,384]{2,1,0:T(8,128)(2,1)S(1)}, bf16[4,264,384]{2,1,0:T(8,128)(2,1)S(1)}, u32[]{:S(2)}, u32[]{:S(2)}) %collective-permute-start) | collective-permute-done | bytes 811040 | tf_op jit(solution)/shard_map/ppermute | solution.py:162
  16.8 2.1 %main.1 = (bf16[128,384]{1,0:T(8,128)(2,1)}, f32[3,128]{1,0:T(4,128)}) custom-call(bf16[4,264,384]{2,1,0:T(8,128)(2,1)S(1)} %bitcast.2, bf16[4,264,384]{2,1,0:T(8,128)(2,1)S(1)} %collective-permute-done.theirs_ref), custom_call_target="tpu_custom_call" | custom-call | tf_op jit(solution)/shard_map/main/pallas_call | solution.py:163
Async XLA Ops:
  14.5 2.3 %collective-permute-start = (bf16[4,264,384]{2,1,0:T(8,128)(2,1)S(1)}, bf16[4,264,384]{2,1,0:T(8,128)(2,1)S(1)}, u32[]{:S(2)}, u32[]{:S(2)}) collective-permute-start(bf16[4,264,384]{2,1,0:T(8,128)(2,1)S(1)} %bitcast.1), channel_id=1, source_target_pairs={{0,4},{4,0},{8,12},{12,8},{16,20},{20,16},{24,28},{28,24},{1,5},{5... | collective-permute-start | bytes 2433032 | tf_op jit(solution)/shard_map/ppermute | solution.py:162

commit v3 on v1

v3 whole, which is shorter than its diff:
```python
import functools

import jax
import jax.numpy as jnp
from jax import lax
from jax.experimental import pallas as pl
from jax.experimental.pallas import tpu as pltpu
from jax.sharding import PartitionSpec as P

EXTRA = 8
VMEM = pltpu.VMEM
ANYWHERE = pl.BlockSpec(memory_space=pl.ANY)
ON_CHIP = pl.BlockSpec(memory_space=VMEM)


def pack_kernel(grad_ref, input_ref, filter_ref, out_ref, filter_vmem, sems):
    rows = grad_ref.shape[0]
    heads, width = filter_ref.shape
    copies = [
        pltpu.make_async_copy(filter_ref, filter_vmem, sems.at[0]),
        pltpu.make_async_copy(grad_ref, out_ref.at[pl.ds(0, rows)], sems.at[1]),
        pltpu.make_async_copy(input_ref, out_ref.at[pl.ds(rows + EXTRA, rows)], sems.at[2]),
    ]
    for copy in copies:
        copy.start()
    copies[0].wait()
    block = filter_vmem[...].astype(jnp.float32)
    block = jnp.concatenate([block, jnp.zeros((EXTRA - heads, width), jnp.float32)], axis=0)
    lags = slice(rows, rows + EXTRA)
    out_ref[lags, :width] = block.astype(out_ref.dtype)
    out_ref[lags, width:] = jnp.zeros((EXTRA, out_ref.shape[1] - width), out_ref.dtype)
    copies[1].wait()
    copies[2].wait()


def repeat(count, step, start):
    if count <= 4:
        for index in range(count):
            start = step(index, start)
        return start
    return lax.fori_loop(0, count, step, start)


def place_in_axis():
    position = lax.axis_index("ctx")
    pair = position // 2
    return position, pair, position - 2 * pair


def lanes_of(head, width):
    return slice(head * width, (head + 1) * width)


def run_of(half):
    return 2 if half % 2 == 0 else 1


def side_by_side(ref, slot, half, rows, lanes):
    return jnp.concatenate([ref[slot + step, rows, lanes] for step in range(run_of(half))], axis=1)


def later(ref, slot, half, rows, lanes):
    parts = []
    for step in range(run_of(half)):
        at = slot + step
        held = ref[jnp.minimum(at, half - 1), rows, lanes]
        parts.append(jnp.where(at < half, held, jnp.zeros_like(held)))
    return jnp.concatenate(parts, axis=1)


def times(left, right):
    return lax.dot_general(left, right, (((1,), (1,)), ((), ())), preferred_element_type=jnp.float32)


def own_kernel(heads, mine_ref, even_ref):
    half, span, channels = mine_ref.shape
    rows = (span - EXTRA) // 2
    width = channels // heads
    _, pair, core = place_in_axis()
    grads, inputs = slice(0, rows), slice(rows + EXTRA, span)
    for head in range(heads):
        lanes = lanes_of(head, width)

        def step(index, total):
            slot = index * run_of(half)
            left = side_by_side(mine_ref, slot, half, inputs, lanes)
            return total + times(left, later(mine_ref, slot + pair + core, half, grads, lanes))

        even_ref[head] = repeat(half // run_of(half), step, jnp.zeros((rows, rows), jnp.float32))


def toeplitz_kernel(heads, mine_ref, grad_ref, toeplitz_ref, lags_ref):
    half, span, _ = mine_ref.shape
    rows = (span - EXTRA) // 2
    blocks = 2 * half
    position, _, core = place_in_axis()
    lags_ref[:, : (blocks + 1) * rows] = jnp.zeros((EXTRA, (blocks + 1) * rows), jnp.float32)

    def place(slot, carry):
        for ref, parity in ((mine_ref, core), (grad_ref, 1 - core)):
            held = ref[slot, rows : rows + EXTRA, :rows]
            at = pl.multiple_of((blocks + 1 + 2 * slot + parity) * rows, rows)
            lags_ref[:, pl.ds(at, rows)] = held.astype(jnp.float32)
        return carry

    repeat(half, place, 0)
    reach = (blocks + 1) * rows
    start = pl.multiple_of((blocks - position) * rows, rows)
    window = lags_ref[:, pl.ds(start, reach)]
    for head in range(heads):
        lines = jnp.broadcast_to(window[head : head + 1], (rows, reach))
        skewed = pltpu.roll(lines, 0, 1, stride=1, stride_axis=0)
        toeplitz_ref[head] = skewed[:, rows:].astype(toeplitz_ref.dtype)


def input_kernel(heads, factor, mine_ref, grad_ref, toeplitz_ref, out_ref, odd_ref):
    half, span, channels = mine_ref.shape
    rows = (span - EXTRA) // 2
    width = channels // heads
    _, pair, core = place_in_axis()
    grads, inputs = slice(0, rows), slice(rows + EXTRA, span)
    for head in range(heads):
        lanes = lanes_of(head, width)

        def gather(slot, total):
            own = pl.multiple_of((2 * slot + core) * rows, rows)
            other = pl.multiple_of((2 * slot + 1 - core) * rows, rows)
            left = jnp.concatenate(
                [toeplitz_ref[head, :, pl.ds(own, rows)], toeplitz_ref[head, :, pl.ds(other, rows)]], axis=1
            )
            both = jnp.concatenate([mine_ref[slot, grads, lanes], grad_ref[slot, grads, lanes]], axis=0)
            return total + jnp.dot(left, both, preferred_element_type=jnp.float32)

        total = repeat(half, gather, jnp.zeros((rows, width), jnp.float32))
        out_ref[:, lanes] = (total * factor).astype(out_ref.dtype)
    for head in range(heads):
        lanes = lanes_of(head, width)

        def step(index, total):
            slot = index * run_of(half)
            left = side_by_side(mine_ref, slot, half, inputs, lanes)
            return total + times(left, later(grad_ref, slot + pair + core, half, grads, lanes))

        odd_ref[head] = repeat(half // run_of(half), step, jnp.zeros((rows, rows), jnp.float32))


def filter_kernel(
    heads, factor, mine_ref, grad_ref, input_ref, even_ref, odd_ref, held_ref, out_ref, terms_ref, terms_vmem, sems
):
    half, rows, channels = input_ref.shape
    width = channels // heads
    _, pair, core = place_in_axis()
    output = pltpu.make_async_copy(held_ref, out_ref, sems.at[0])
    output.start()
    whole = slice(0, rows)
    sums = []
    for head in range(heads):
        lanes = lanes_of(head, width)

        def step(index, total):
            slot = index * run_of(half)
            left = side_by_side(input_ref, slot, half, whole, lanes)
            right = jnp.concatenate(
                [
                    later(grad_ref, slot + pair + core, half, whole, lanes),
                    later(mine_ref, slot + pair + 1 - core, half, whole, lanes),
                ],
                axis=0,
            )
            return total + times(left, right)

        products = repeat(half // run_of(half), step, jnp.zeros((rows, 2 * rows), jnp.float32))
        even = products[:, :rows] + even_ref[head]
        odd = products[:, rows:] + odd_ref[head]
        products = jnp.concatenate([jnp.where(core == 0, even, odd), jnp.where(core == 0, odd, even)], axis=1)
        folded = products[0:8]
        for group in range(1, rows // 8):
            folded = folded + pltpu.roll(products[8 * group : 8 * group + 8], 2 * rows - 8 * group, 1)
        sums.append(folded)
    folded = jnp.concatenate(sums, axis=0)
    line = lax.broadcasted_iota(jnp.int32, folded.shape, 0)
    for bit in (1, 2, 4):
        folded = jnp.where((line & bit) != 0, pltpu.roll(folded, 2 * rows - bit, 1), folded)
    for head in range(heads):
        terms_vmem[head : head + 1, :] = jnp.sum(folded[8 * head : 8 * head + 8, :rows], axis=0, keepdims=True) * factor
    terms = pltpu.make_async_copy(terms_vmem, terms_ref, sems.at[1])
    terms.start()
    output.wait()
    terms.wait()


def call(kernel, name, args, out_shape, out_specs, scratch=(), scratch_bytes=0, in_specs=None, micros=1.0):
    return pl.pallas_call(
        kernel,
        out_shape=out_shape,
        in_specs=in_specs or [ON_CHIP] * len(args),
        out_specs=out_specs,
        scratch_shapes=list(scratch),
        compiler_params=pltpu.CompilerParams(vmem_limit_bytes=min(scratch_bytes + (4 << 20), 60 << 20)),
        cost_estimate=pl.CostEstimate(flops=int(micros * 1e9), bytes_accessed=int(micros * 3e6), transcendentals=0),
        name=name,
    )(*args)


def body(inputs, grad_out, filter_w):
    rows, channels = inputs.shape
    heads = filter_w.shape[0]
    blocks = lax.axis_size("ctx")
    half = blocks // 2
    factor = float(rows * blocks) ** (-0.5)
    kind = inputs.dtype
    span = 2 * rows + EXTRA
    shape = jax.ShapeDtypeStruct
    swaps = [(index, index ^ 1) for index in range(blocks)]
    payload = call(
        pack_kernel,
        "pack",
        [pltpu.with_memory_space_constraint(each, pltpu.HBM) for each in (grad_out, inputs, filter_w)],
        shape((span, channels), kind),
        ON_CHIP,
        [VMEM(filter_w.shape, filter_w.dtype), pltpu.SemaphoreType.DMA((3,))],
        in_specs=[pl.BlockSpec(memory_space=pltpu.HBM)] * 3,
    )
    groups = [[2 * slot + core for slot in range(half)] for core in range(2)]
    mine = lax.all_gather(payload, "ctx", axis=0, tiled=False, axis_index_groups=groups)
    grads = lax.ppermute(mine[:, : rows + EXTRA], "ctx", swaps)
    others = lax.ppermute(mine[:, rows + EXTRA :], "ctx", swaps)
    square = shape((heads, rows, rows), jnp.float32)
    even = call(functools.partial(own_kernel, heads), "own", [mine], square, ON_CHIP)
    toeplitz = call(
        functools.partial(toeplitz_kernel, heads),
        "toeplitz",
        [mine, grads],
        shape((heads, rows, blocks * rows), kind),
        ON_CHIP,
        [VMEM((EXTRA, (2 * blocks + 1) * rows), jnp.float32)],
        4 * EXTRA * (2 * blocks + 1) * rows,
    )
    held, odd = call(
        functools.partial(input_kernel, heads, factor),
        "input",
        [mine, grads, toeplitz],
        (shape((rows, channels), kind), square),
        (ON_CHIP, ON_CHIP),
    )
    return call(
        functools.partial(filter_kernel, heads, factor),
        "filter",
        [mine, grads, others, even, odd, held],
        (shape((rows, channels), kind), shape((heads, rows), jnp.float32)),
        (ANYWHERE, ANYWHERE),
        [VMEM((heads, rows), jnp.float32), pltpu.SemaphoreType.DMA((2,))],
    )


def solution(mesh):
    placed = (P("ctx", "ch"), P("ctx", "ch"), P("ch", "ctx"))
    return jax.shard_map(
        body,
        mesh=mesh,
        in_specs=placed,
        out_specs=(P("ctx", "ch"), P("ch", "ctx")),
        check_vma=False,
    )
```

time: 23.3 us -> 18.7 us (0.80)
  Pallas kernels: 5.14 us -> 3.4 us
  waiting for transfers between devices: 2.32 us -> 0.86 us
  blocking collectives: 14.1 us -> 12.9 us
  local copies, waits for them, and re-layouts: 0.9 us -> 0.08 us
  starting transfers between devices: 0.01 us -> 0.63 us
    pallas_call x2 -> x5, Pallas kernels: 5.14 us -> 3.4 us  [call(): pl.pallas_call(kernel, out_shape=out_shape, in_specs=in_specs or [ON_CHIP...]
    ppermute x1 -> x2, waiting for transfers between devices: 2.32 us -> 0.86 us  [the longest x1 0.85 us: body(): grads = lax.ppermute(mine[:, :rows + EXTRA], 'ctx', swaps)]
    all_gather x1, blocking collectives: 14.1 us -> 12.9 us  [body(): lax.all_gather(payload, 'ctx', axis=0, tiled=False, axis_index_groups=gro...]
    unnamed x4 -> x0, local copies, waits for them, and re-layouts: 0.9 us -> none
    ppermute x1 -> x2, starting transfers between devices: 0.01 us -> 0.63 us  [the longest x1 0.56 us: body(): others = lax.ppermute(mine[:, rows + EXTRA:], 'ctx', swaps)]
  transfers between devices with their start and end apart: 1 -> 2, of which waited for: 1 -> 1; matrix products, arithmetic and copies ran while one was open for 0% -> 0% of each run, Pallas kernels for 0% -> 6%
where the time goes in v3:
time: 18.7 us; the launch traced here: 18.6 us
  blocking collectives  12.9 us (69%)
  Pallas kernels  3.4 us (18%)
  waiting for transfers between devices  0.86 us (5%)
  between operations  0.69 us (4%)
  starting transfers between devices  0.63 us (3%)
    all_gather x1, blocking collectives, body(): lax.all_gather(payload, 'ctx', axis=0, tiled=False, axis_index_groups=gro...  12.9 us
    pallas_call x5, Pallas kernels, call(): pl.pallas_call(kernel, out_shape=out_shape, in_specs=in_specs or [ON_CHIP...  3.4 us
    ppermute x1, waiting for transfers between devices, body(): grads = lax.ppermute(mine[:, :rows + EXTRA], 'ctx', swaps)  0.85 us
    ppermute x1, starting transfers between devices, body(): others = lax.ppermute(mine[:, rows + EXTRA:], 'ctx', swaps)  0.56 us
  transfers between devices with their start and end apart: 2, of which 1 were waited for; matrix products, arithmetic and copies ran while one was open for 0% of the time, Pallas kernels for 6%

profile of v3, /device:TPU:0, one launch (start us, length us, event | category | flops | bytes accessed | tf_op | source)
XLA Modules:
  0.0 18.6 jit_solution(3861239467645423432)
XLA Ops:
  0.6 1.0 %pack.1 = bf16[264,384]{1,0:T(8,128)(2,1)S(1)} custom-call(bf16[128,384]{1,0:T(8,128)(2,1)} %grad_ref.1, bf16[128,384]{1,0:T(8,128)(2,1)} %input_ref.1, bf16[3,128]{1,0:T(4,128)(2,1)} %filter_ref.1), custom_call_target="tpu_custom_call" | custom-call | flops 1000000000 | bytes 3000000 | tf_op jit(solution)/shard_map/pack/pallas_call | solution.py:193
  1.6 12.9 %all-gather = bf16[1056,384]{1,0:T(8,128)(2,1)S(1)} all-gather(bf16[264,384]{1,0:T(8,128)(2,1)S(1)} %pack.1), channel_id=2, replica_groups={{0,8,16,24},{4,12,20,28},{1,9,17,25},{5,13,21,29},{2,10,18,26},{6,14,22..., dimensions={0}, use_global_device_ids=true | all-gather | bytes 1013760 | tf_op jit(solution)/shard_map/all_gather | solution.py:225
  14.6 0.1 collective-permute-start
  14.7 0.6 %collective-permute-start.1 = (bf16[4,128,384]{2,1,0:T(8,128)(2,1)S(1)}, bf16[4,128,384]{2,1,0:T(8,128)(2,1)S(1)}, u32[]{:S(2)}, u32[]{:S(2)}) collective-permute-start(bf16[4,128,384]{2,1,0:T(8,128)(2,1)S(1)} %slice.9), channel_id=1, source_target_pairs={{0,4},{4,0},{8,12},{12,8},{16,20},{20,16},{24,28},{28,24},{1,5},{5... | collective-permute-start | bytes 1179656 | tf_op jit(solution)/shard_map/ppermute | solution.py:227
  15.2 0.3 %own.1.even_ref = f32[3,128,128]{2,1,0:T(8,128)S(1)} custom-call(bf16[4,264,384]{2,1,0:T(8,128)(2,1)S(1)} %bitcast.3), custom_call_target="tpu_custom_call" | custom-call | flops 1000000000 | bytes 3000000 | tf_op jit(solution)/shard_map/own/pallas_call | solution.py:193
  15.5 0.9 %collective-permute-done.grad_ref = bf16[4,136,384]{2,1,0:T(8,128)(2,1)S(1)} collective-permute-done((bf16[4,136,384]{2,1,0:T(8,128)(2,1)S(1)}, bf16[4,136,384]{2,1,0:T(8,128)(2,1)S(1)}, u32[]{:S(2)}, u32[]{:S(2)}) %collective-permute-start) | collective-permute-done | bytes 417824 | tf_op jit(solution)/shard_map/ppermute | solution.py:226
  16.4 0.3 %toeplitz.1.toeplitz_ref = bf16[3,128,1024]{2,1,0:T(8,128)(2,1)S(1)} custom-call(bf16[4,264,384]{2,1,0:T(8,128)(2,1)S(1)} %bitcast.4, bf16[4,136,384]{2,1,0:T(8,128)(2,1)S(1)} %collective-permute-done.grad_ref), custom_call_target="tpu_custom_call" | custom-call | flops 1000000000 | bytes 3000000 | tf_op jit(solution)/shard_map/toeplitz/pallas_call | solution.py:193
  16.7 0.5 %input.1 = (bf16[128,384]{1,0:T(8,128)(2,1)S(1)}, f32[3,128,128]{2,1,0:T(8,128)S(1)}) custom-call(bf16[4,264,384]{2,1,0:T(8,128)(2,1)S(1)} %bitcast.5, bf16[4,136,384]{2,1,0:T(8,128)(2,1)S(1)} %collective-permute-done.grad_ref, bf16[3,128,1024]{2,1,0:T(8,128)(2,1)S(1)} %toeplitz.1.toeplitz_ref), custom_call_target="tpu_custom_call" | custom-call | flops 1000000000 | bytes 3000000 | tf_op jit(solution)/shard_map/input/pallas_call | solution.py:193
  17.2 0.0 collective-permute-done.1.input_ref
  17.2 1.3 %filter.1 = (bf16[128,384]{1,0:T(8,128)(2,1)}, f32[3,128]{1,0:T(4,128)}) custom-call(bf16[4,264,384]{2,1,0:T(8,128)(2,1)S(1)} %bitcast.6, bf16[4,136,384]{2,1,0:T(8,128)(2,1)S(1)} %collective-permute-done.grad_ref, bf16[4,128,384]{2,1,0:T(8,128)(2,1)S(1)} %collective-permute-done.1.input_ref, f32[3,128,128]{2,1,0:T(8,128)S(1)} %own.1.even_ref, ...), custom_call_target="tpu_custom_call" | custom-call | flops 1000000000 | bytes 3000000 | tf_op jit(solution)/shard_map/filter/pallas_call | solution.py:193
  (2 shorter events, 0.1 us)
Async XLA Ops:
  14.6 1.8 %collective-permute-start = (bf16[4,136,384]{2,1,0:T(8,128)(2,1)S(1)}, bf16[4,136,384]{2,1,0:T(8,128)(2,1)S(1)}, u32[]{:S(2)}, u32[]{:S(2)}) collective-permute-start(bf16[4,136,384]{2,1,0:T(8,128)(2,1)S(1)} %slice.8), channel_id=1, source_target_pairs={{0,4},{4,0},{8,12},{12,8},{16,20},{20,16},{24,28},{28,24},{1,5},{5... | collective-permute-start | bytes 1253384 | tf_op jit(solution)/shard_map/ppermute | solution.py:226
  14.7 2.5 %collective-permute-start.1 = (bf16[4,128,384]{2,1,0:T(8,128)(2,1)S(1)}, bf16[4,128,384]{2,1,0:T(8,128)(2,1)S(1)}, u32[]{:S(2)}, u32[]{:S(2)}) collective-permute-start(bf16[4,128,384]{2,1,0:T(8,128)(2,1)S(1)} %slice.9), channel_id=1, source_target_pairs={{0,4},{4,0},{8,12},{12,8},{16,20},{20,16},{24,28},{28,24},{1,5},{5... | collective-permute-start | bytes 1179656 | tf_op jit(solution)/shard_map/ppermute | solution.py:227

commit v4 on v3

--- a/solution.py
+++ b/solution.py
@@ -7,7 +7,9 @@
 from jax.experimental.pallas import tpu as pltpu
 from jax.sharding import PartitionSpec as P
 
+
 EXTRA = 8
+PIECES = 2
 VMEM = pltpu.VMEM
 ANYWHERE = pl.BlockSpec(memory_space=pl.ANY)
 ON_CHIP = pl.BlockSpec(memory_space=VMEM)
@@ -16,11 +18,13 @@
 def pack_kernel(grad_ref, input_ref, filter_ref, out_ref, filter_vmem, sems):
     rows = grad_ref.shape[0]
     heads, width = filter_ref.shape
-    copies = [
-        pltpu.make_async_copy(filter_ref, filter_vmem, sems.at[0]),
-        pltpu.make_async_copy(grad_ref, out_ref.at[pl.ds(0, rows)], sems.at[1]),
-        pltpu.make_async_copy(input_ref, out_ref.at[pl.ds(rows + EXTRA, rows)], sems.at[2]),
-    ]
+    copies = [pltpu.make_async_copy(filter_ref, filter_vmem, sems.at[0])]
+    piece = rows // PIECES
+    for at in range(PIECES):
+        part = pl.ds(at * piece, piece)
+        copies.append(pltpu.make_async_copy(grad_ref.at[part], out_ref.at[part], sems.at[1 + 2 * at]))
+        into = pl.ds(rows + EXTRA + at * piece, piece)
+        copies.append(pltpu.make_async_copy(input_ref.at[part], out_ref.at[into], sems.at[2 + 2 * at]))
     for copy in copies:
         copy.start()
     copies[0].wait()
@@ -29,8 +33,8 @@
     lags = slice(rows, rows + EXTRA)
     out_ref[lags, :width] = block.astype(out_ref.dtype)
     out_ref[lags, width:] = jnp.zeros((EXTRA, out_ref.shape[1] - width), out_ref.dtype)
-    copies[1].wait()
-    copies[2].wait()
+    for copy in copies[1:]:
+        copy.wait()
 
 
 def repeat(count, step, start):
@@ -52,7 +56,7 @@
 
 
 def run_of(half):
-    return 2 if half % 2 == 0 else 1
+    return next(run for run in (4, 2, 1) if half % run == 0)
 
 
 def side_by_side(ref, slot, half, rows, lanes):
@@ -89,7 +93,7 @@
         even_ref[head] = repeat(half // run_of(half), step, jnp.zeros((rows, rows), jnp.float32))
 
 
-def toeplitz_kernel(heads, mine_ref, grad_ref, toeplitz_ref, lags_ref):
+def toeplitz_kernel(heads, mine_ref, filter_ref, toeplitz_ref, lags_ref):
     half, span, _ = mine_ref.shape
     rows = (span - EXTRA) // 2
     blocks = 2 * half
@@ -97,8 +101,7 @@
     lags_ref[:, : (blocks + 1) * rows] = jnp.zeros((EXTRA, (blocks + 1) * rows), jnp.float32)
 
     def place(slot, carry):
-        for ref, parity in ((mine_ref, core), (grad_ref, 1 - core)):
-            held = ref[slot, rows : rows + EXTRA, :rows]
+        for held, parity in ((mine_ref[slot, rows : rows + EXTRA, :rows], core), (filter_ref[slot], 1 - core)):
             at = pl.multiple_of((blocks + 1 + 2 * slot + parity) * rows, rows)
             lags_ref[:, pl.ds(at, rows)] = held.astype(jnp.float32)
         return carry
@@ -108,9 +111,9 @@
     start = pl.multiple_of((blocks - position) * rows, rows)
     window = lags_ref[:, pl.ds(start, reach)]
     for head in range(heads):
-        lines = jnp.broadcast_to(window[head : head + 1], (rows, reach))
+        lines = jnp.broadcast_to(window[head : head + 1], (rows, reach)).astype(toeplitz_ref.dtype)
         skewed = pltpu.roll(lines, 0, 1, stride=1, stride_axis=0)
-        toeplitz_ref[head] = skewed[:, rows:].astype(toeplitz_ref.dtype)
+        toeplitz_ref[head] = skewed[:, rows:]
 
 
 def input_kernel(heads, factor, mine_ref, grad_ref, toeplitz_ref, out_ref, odd_ref):
@@ -178,18 +181,19 @@
             folded = folded + pltpu.roll(products[8 * group : 8 * group + 8], 2 * rows - 8 * group, 1)
         sums.append(folded)
     folded = jnp.concatenate(sums, axis=0)
-    line = lax.broadcasted_iota(jnp.int32, folded.shape, 0)
-    for bit in (1, 2, 4):
-        folded = jnp.where((line & bit) != 0, pltpu.roll(folded, 2 * rows - bit, 1), folded)
-    for head in range(heads):
-        terms_vmem[head : head + 1, :] = jnp.sum(folded[8 * head : 8 * head + 8, :rows], axis=0, keepdims=True) * factor
-    terms = pltpu.make_async_copy(terms_vmem, terms_ref, sems.at[1])
-    terms.start()
+    line = lax.broadcasted_iota(jnp.int32, folded.shape, 0) & 7
+    terms = jnp.where(line == 0, folded, 0.0)
+    for shift in range(1, 8):
+        terms = terms + jnp.where(line == shift, pltpu.roll(folded, 2 * rows - shift, 1), 0.0)
+    for head in range(heads):
+        terms_vmem[head : head + 1, :] = jnp.sum(terms[8 * head : 8 * head + 8, :rows], axis=0, keepdims=True) * factor
+    last = pltpu.make_async_copy(terms_vmem, terms_ref, sems.at[1])
+    last.start()
     output.wait()
-    terms.wait()
-
-
-def call(kernel, name, args, out_shape, out_specs, scratch=(), scratch_bytes=0, in_specs=None, micros=1.0):
+    last.wait()
+
+
+def call(kernel, args, out_shape, out_specs, scratch=(), scratch_bytes=0, in_specs=None, micros=1.0):
     return pl.pallas_call(
         kernel,
         out_shape=out_shape,
@@ -198,7 +202,6 @@
         scratch_shapes=list(scratch),
         compiler_params=pltpu.CompilerParams(vmem_limit_bytes=min(scratch_bytes + (4 << 20), 60 << 20)),
         cost_estimate=pl.CostEstimate(flops=int(micros * 1e9), bytes_accessed=int(micros * 3e6), transcendentals=0),
-        name=name,
     )(*args)
 
 
@@ -214,23 +217,22 @@
     swaps = [(index, index ^ 1) for index in range(blocks)]
     payload = call(
         pack_kernel,
-        "pack",
         [pltpu.with_memory_space_constraint(each, pltpu.HBM) for each in (grad_out, inputs, filter_w)],
         shape((span, channels), kind),
         ON_CHIP,
-        [VMEM(filter_w.shape, filter_w.dtype), pltpu.SemaphoreType.DMA((3,))],
+        [VMEM(filter_w.shape, filter_w.dtype), pltpu.SemaphoreType.DMA((1 + 2 * PIECES,))],
         in_specs=[pl.BlockSpec(memory_space=pltpu.HBM)] * 3,
     )
     groups = [[2 * slot + core for slot in range(half)] for core in range(2)]
     mine = lax.all_gather(payload, "ctx", axis=0, tiled=False, axis_index_groups=groups)
-    grads = lax.ppermute(mine[:, : rows + EXTRA], "ctx", swaps)
+    filters = lax.ppermute(mine[:, rows : rows + EXTRA, :rows], "ctx", swaps)
+    grads = lax.ppermute(mine[:, :rows], "ctx", swaps)
     others = lax.ppermute(mine[:, rows + EXTRA :], "ctx", swaps)
     square = shape((heads, rows, rows), jnp.float32)
-    even = call(functools.partial(own_kernel, heads), "own", [mine], square, ON_CHIP)
+    even = call(functools.partial(own_kernel, heads), [mine], square, ON_CHIP)
     toeplitz = call(
         functools.partial(toeplitz_kernel, heads),
-        "toeplitz",
-        [mine, grads],
+        [mine, filters],
         shape((heads, rows, blocks * rows), kind),
         ON_CHIP,
         [VMEM((EXTRA, (2 * blocks + 1) * rows), jnp.float32)],
@@ -238,14 +240,12 @@
     )
     held, odd = call(
         functools.partial(input_kernel, heads, factor),
-        "input",
         [mine, grads, toeplitz],
         (shape((rows, channels), kind), square),
         (ON_CHIP, ON_CHIP),
     )
     return call(
         functools.partial(filter_kernel, heads, factor),
-        "filter",
         [mine, grads, others, even, odd, held],
         (shape((rows, channels), kind), shape((heads, rows), jnp.float32)),
         (ANYWHERE, ANYWHERE),

time: 18.7 us -> 19.2 us (1.027)
  waiting for transfers between devices: 0.86 us -> 1.42 us
    ppermute x1 -> x2, waiting for transfers between devices: 0.85 us -> 1.42 us  [the longest x1 1.42 us: body(): filters = lax.ppermute(mine[:, rows:rows + EXTRA, :rows], 'ctx', swaps)]
  transfers between devices with their start and end apart: 2 -> 3, of which waited for: 1 -> 1; matrix products, arithmetic and copies ran while one was open for 0% -> 0% of each run, Pallas kernels for 6% -> 6%
where the time goes in v4:
time: 19.2 us; the launch traced here: 19 us
  blocking collectives  12.9 us (67%)
  Pallas kernels  3.23 us (17%)
  waiting for transfers between devices  1.42 us (7%)
  between operations  0.69 us (4%)
  starting transfers between devices  0.65 us (3%)
    all_gather x1, blocking collectives, body(): lax.all_gather(payload, 'ctx', axis=0, tiled=False, axis_index_groups=gro...  12.9 us
    pallas_call x5, Pallas kernels, call(): pl.pallas_call(kernel, out_shape=out_shape, in_specs=in_specs or [ON_CHIP...  3.23 us
    ppermute x1, waiting for transfers between devices, body(): filters = lax.ppermute(mine[:, rows:rows + EXTRA, :rows], 'ctx', swaps)  1.42 us
    ppermute x1, starting transfers between devices, body(): others = lax.ppermute(mine[:, rows + EXTRA:], 'ctx', swaps)  0.5 us
  transfers between devices with their start and end apart: 3, of which 1 were waited for; matrix products, arithmetic and copies ran while one was open for 0% of the time, Pallas kernels for 6%

profile of v4, /device:TPU:0, one launch (start us, length us, event | category | flops | bytes accessed | tf_op | source)
XLA Modules:
  0.0 19.0 jit_solution(16976153544019663647)
XLA Ops:
  0.6 0.9 %shard_map.50 = bf16[264,384]{1,0:T(8,128)(2,1)S(1)} custom-call(bf16[128,384]{1,0:T(8,128)(2,1)} %grad_ref.1, bf16[128,384]{1,0:T(8,128)(2,1)} %input_ref.1, bf16[3,128]{1,0:T(4,128)(2,1)} %filter_ref.1), custom_call_target="tpu_custom_call" | custom-call | flops 1000000000 | bytes 3000000 | tf_op jit(solution)/shard_map/pallas_call | solution.py:197
  1.6 12.9 %all-gather = bf16[1056,384]{1,0:T(8,128)(2,1)S(1)} all-gather(bf16[264,384]{1,0:T(8,128)(2,1)S(1)} %shard_map.50), channel_id=2, replica_groups={{0,8,16,24},{4,12,20,28},{1,9,17,25},{5,13,21,29},{2,10,18,26},{6,14,22..., dimensions={0}, use_global_device_ids=true | all-gather | bytes 1013760 | tf_op jit(solution)/shard_map/all_gather | solution.py:227
  14.5 0.1 fusion
  14.6 0.1 collective-permute-start
  14.6 0.5 %collective-permute-start.1 = (bf16[4,128,384]{2,1,0:T(8,128)(2,1)S(1)}, bf16[4,128,384]{2,1,0:T(8,128)(2,1)S(1)}, u32[]{:S(2)}, u32[]{:S(2)}) collective-permute-start(bf16[4,128,384]{2,1,0:T(8,128)(2,1)S(1)} %get-tuple-element.6), channel_id=1, source_target_pairs={{0,4},{4,0},{8,12},{12,8},{16,20},{20,16},{24,28},{28,24},{1,5},{5... | collective-permute-start | bytes 1179656 | tf_op jit(solution)/shard_map/ppermute | solution.py:230
  15.1 0.1 collective-permute-start.2
  15.2 0.3 %shard_map.51.even_ref = f32[3,128,128]{2,1,0:T(8,128)S(1)} custom-call(bf16[4,264,384]{2,1,0:T(8,128)(2,1)S(1)} %bitcast.3), custom_call_target="tpu_custom_call" | custom-call | flops 1000000000 | bytes 3000000 | tf_op jit(solution)/shard_map/pallas_call | solution.py:197
  15.5 1.4 %collective-permute-done.2.filter_ref = bf16[4,8,128]{2,1,0:T(8,128)(2,1)S(1)} collective-permute-done((bf16[4,8,128]{2,1,0:T(8,128)(2,1)S(1)}, bf16[4,8,128]{2,1,0:T(8,128)(2,1)S(1)}, u32[]{:S(2)}, u32[]{:S(2)}) %collective-permute-start.2) | collective-permute-done | bytes 8224 | tf_op jit(solution)/shard_map/ppermute | solution.py:228
  16.9 0.3 %shard_map.52.toeplitz_ref = bf16[3,128,1024]{2,1,0:T(8,128)(2,1)S(1)} custom-call(bf16[4,264,384]{2,1,0:T(8,128)(2,1)S(1)} %bitcast.4, bf16[4,8,128]{2,1,0:T(8,128)(2,1)S(1)} %collective-permute-done.2.filter_ref), custom_call_target="tpu_custom_call" | custom-call | flops 1000000000 | bytes 3000000 | tf_op jit(solution)/shard_map/pallas_call | solution.py:197
  17.2 0.0 collective-permute-done.grad_ref
  17.2 0.5 %shard_map.53 = (bf16[128,384]{1,0:T(8,128)(2,1)S(1)}, f32[3,128,128]{2,1,0:T(8,128)S(1)}) custom-call(bf16[4,264,384]{2,1,0:T(8,128)(2,1)S(1)} %bitcast.5, bf16[4,128,384]{2,1,0:T(8,128)(2,1)S(1)} %collective-permute-done.grad_ref, bf16[3,128,1024]{2,1,0:T(8,128)(2,1)S(1)} %shard_map.52.toeplitz_ref), custom_call_target="tpu_custom_call" | custom-call | flops 1000000000 | bytes 3000000 | tf_op jit(solution)/shard_map/pallas_call | solution.py:197
  17.7 0.0 collective-permute-done.1.input_ref
  17.8 1.2 %shard_map.54 = (bf16[128,384]{1,0:T(8,128)(2,1)}, f32[3,128]{1,0:T(4,128)}) custom-call(bf16[4,264,384]{2,1,0:T(8,128)(2,1)S(1)} %bitcast.6, bf16[4,128,384]{2,1,0:T(8,128)(2,1)S(1)} %collective-permute-done.grad_ref, bf16[4,128,384]{2,1,0:T(8,128)(2,1)S(1)} %collective-permute-done.1.input_ref, f32[3,128,128]{2,1,0:T(8,128)S(1)} %shard_map.51.even_ref, ...), custom_call_target="tpu_custom_call" | custom-call | flops 1000000000 | bytes 3000000 | tf_op jit(solution)/shard_map/pallas_call | solution.py:197
  (1 shorter events, 0.0 us)
Async XLA Ops:
  14.6 2.7 %collective-permute-start = (bf16[4,128,384]{2,1,0:T(8,128)(2,1)S(1)}, bf16[4,128,384]{2,1,0:T(8,128)(2,1)S(1)}, u32[]{:S(2)}, u32[]{:S(2)}) collective-permute-start(bf16[4,128,384]{2,1,0:T(8,128)(2,1)S(1)} %get-tuple-element.7), channel_id=1, source_target_pairs={{0,4},{4,0},{8,12},{12,8},{16,20},{20,16},{24,28},{28,24},{1,5},{5... | collective-permute-start | bytes 1179656 | tf_op jit(solution)/shard_map/ppermute | solution.py:229
  14.6 3.1 %collective-permute-start.1 = (bf16[4,128,384]{2,1,0:T(8,128)(2,1)S(1)}, bf16[4,128,384]{2,1,0:T(8,128)(2,1)S(1)}, u32[]{:S(2)}, u32[]{:S(2)}) collective-permute-start(bf16[4,128,384]{2,1,0:T(8,128)(2,1)S(1)} %get-tuple-element.6), channel_id=1, source_target_pairs={{0,4},{4,0},{8,12},{12,8},{16,20},{20,16},{24,28},{28,24},{1,5},{5... | collective-permute-start | bytes 1179656 | tf_op jit(solution)/shard_map/ppermute | solution.py:230
  15.1 1.8 %collective-permute-start.2 = (bf16[4,8,128]{2,1,0:T(8,128)(2,1)S(1)}, bf16[4,8,128]{2,1,0:T(8,128)(2,1)S(1)}, u32[]{:S(2)}, u32[]{:S(2)}) collective-permute-start(bf16[4,8,128]{2,1,0:T(8,128)(2,1)S(1)} %slice.14), channel_id=1, source_target_pairs={{0,4},{4,0},{8,12},{12,8},{16,20},{20,16},{24,28},{28,24},{1,5},{5... | collective-permute-start | bytes 24584 | tf_op jit(solution)/shard_map/ppermute | solution.py:228
